TPU v7x, 32 devices: a whole 2x2x4 slice. The times are simulated.
32 devices in a mesh: group: 4 (over x, core), seq: 8 (over z, y).
Axes of the slice: x: 2, y: 2, z: 4, core: 2. Of those that a mesh axis runs over, the one named last changes fastest.
Arguments:
- tokens: bfloat16 [4, 1024, 2048], P('group', 'seq'), may hold values from -6 to 6
- norm_gain: bfloat16 [2048], replicated, may hold values from 0.25 to 1.75
- w_qkv: bfloat16 [2048, 1920], P(('group', 'seq')), may hold values from -1.767767 to 1.767767
- prefix_kv: bfloat16 [4, 512, 640], P('group', 'seq'), may hold values from -12 to 12
- segments: int32 [4, 1024], P('group', 'seq'), may hold values from 0 to 3, never falling along the last dimension, each value on 1 to 512 neighbouring positions
Outputs:
- context: bfloat16 [4, 1024, 1280], P('group', 'seq')
Inputs may be any that keep to these rules, and one draw needn't show every extreme that they name: `segments`: within each group's 1024 suffix tokens the request numbers never fall; every request holds 1 to 512 tokens and one holds exactly 512.
All inputs are finite; a program needn't handle non-finite values.
Results may differ from a plain program's by a relative error of at most 0.0096.
Values may be sent and summed in bfloat16 or wider, within the bound.
No kernel may reach another device: no remote copies, remote signals or barrier semaphores. Data moves between devices by JAX's collectives and lax.ppermute only.
A program may use at most 64 MiB of HBM per device.

v0:
```python
import math
import jax
import jax.numpy as jnp
from jax import lax
from jax.sharding import PartitionSpec as P

HD = 64
QW = 1280
KVW = 320


def body(tokens, norm_gain, w_qkv, prefix_kv, segments):
    inputs = tokens[0]
    seg_ids = segments[0]
    row_count = inputs.shape[0]
    key_heads = KVW // HD
    repeats = QW // KVW
    values_f = inputs.astype(jnp.float32)
    mean_square = jnp.mean(values_f * values_f, axis=-1, keepdims=True)
    normed = (values_f * lax.rsqrt(mean_square + 1e-05) * norm_gain.astype(jnp.float32)).astype(
        jnp.bfloat16
    )
    folded = jnp.dot(
        normed,
        lax.all_gather(w_qkv, ("group", "seq"), axis=0, tiled=True),
        preferred_element_type=jnp.float32,
    )
    projected = folded.astype(jnp.bfloat16)
    queries = projected[:, :QW].reshape(row_count, key_heads, repeats, HD)
    local_kv = projected[:, QW:]

    def absorb(softmax_state, keyvals, visible):
        running_max, denominator, numerator = softmax_state
        key_count = keyvals.shape[0]
        key_part = keyvals[:, :KVW].reshape(key_count, key_heads, HD)
        value_part = keyvals[:, KVW:].reshape(key_count, key_heads, HD)
        scores = (
            jnp.einsum("tgrd,ngd->tgrn", queries, key_part, preferred_element_type=jnp.float32)
            * 0.125
        )
        if visible is not None:
            scores = jnp.where(visible[:, None, None, :], scores, jnp.float32(-1e30))
        new_max = jnp.maximum(running_max, jnp.max(scores, axis=-1))
        probability = jnp.exp(scores - new_max[..., None])
        if visible is not None:
            probability = jnp.where(visible[:, None, None, :], probability, jnp.float32(0.0))
        factor = jnp.exp(running_max - new_max)
        denominator = denominator * factor + jnp.sum(probability, axis=-1)
        numerator = numerator * factor[..., None] + jnp.einsum(
            "tgrn,ngd->tgrd",
            probability.astype(jnp.bfloat16),
            value_part,
            preferred_element_type=jnp.float32,
        )
        return (new_max, denominator, numerator)

    def sweep_keys(softmax_state, keyvals, key_seg, first_row, build):
        key_count = keyvals.shape[0]
        block_len = math.gcd(key_count, 512)
        if block_len == key_count:
            return absorb(softmax_state, keyvals, build(key_seg, first_row))

        def block_step(block_index, running):
            key_start = block_index * block_len
            keys_block = lax.dynamic_slice_in_dim(keyvals, key_start, block_len, 0)
            if key_seg is None:
                seg_block = None
            else:
                seg_block = lax.dynamic_slice_in_dim(key_seg, key_start, block_len, 0)
            return absorb(running, keys_block, build(seg_block, key_start))

        return lax.fori_loop(0, key_count // block_len, block_step, softmax_state)

    start_state = (
        jnp.full((row_count, key_heads, repeats), -1e30, jnp.float32),
        jnp.zeros((row_count, key_heads, repeats), jnp.float32),
        jnp.zeros((row_count, key_heads, repeats, HD), jnp.float32),
    )

    def open_rows(seg_block, key_start):
        return None

    softmax_state = sweep_keys(
        start_state,
        lax.all_gather(prefix_kv[0], "seq", axis=0, tiled=True),
        None,
        jnp.int32(0),
        open_rows,
    )
    query_pos = lax.axis_index("seq") * row_count + jnp.arange(row_count, dtype=jnp.int32)

    def causal_rows(seg_block, key_start):
        key_pos = key_start + jnp.arange(seg_block.shape[0], dtype=jnp.int32)
        return (seg_block[None, :] == seg_ids[:, None]) & (key_pos[None, :] <= query_pos[:, None])

    keyvals = lax.all_gather(local_kv, "seq", axis=0, tiled=True)
    key_seg = lax.all_gather(seg_ids, "seq", axis=0, tiled=True)
    softmax_state = sweep_keys(softmax_state, keyvals, key_seg, jnp.int32(0), causal_rows)
    running_max, denominator, numerator = softmax_state
    context = (numerator / denominator[..., None]).reshape(row_count, QW).astype(jnp.bfloat16)
    return context[None]


def solution(mesh):
    return jax.shard_map(
        body,
        mesh=mesh,
        in_specs=(
            P("group", "seq", None),
            P(),
            P(("group", "seq"), None),
            P("group", "seq", None),
            P("group", "seq"),
        ),
        out_specs=P("group", "seq", None),
        check_vma=False,
    )
```

profile of v0, /device:TPU:0, one launch (start us, length us, event | category | flops | bytes accessed | tf_op | source)
XLA Modules:
  0.0 169.5 jit_solution(7326391197680316243)
XLA Ops:
  6.5 0.7 all-gather.5.cloned.1.call-update
  7.3 0.7 convert_element_type.40
  8.0 1.2 fusion.30
  9.2 79.2 %all-gather.5.cloned.1.call-done = bf16[2048,1920]{1,0:T(8,128)(2,1)} async-done(((bf16[64,1920]{1,0:T(8,128)(2,1)}), bf16[2048,1920]{1,0:T(8,128)(2,1)}) %all-gather.5.cloned.1.call-update) | async-done | bytes 7864336 | tf_op jit(solution)/shard_map/all_gather | solution.py:25
  88.4 4.7 %convolution_convert_fusion = bf16[128,1920]{1,0:T(8,128)(2,1)S(1)} fusion(bf16[2048,1920]{1,0:T(8,128)(2,1)} %all-gather.5.cloned.1.call-done, bf16[1,128,2048]{2,1,0:T(8,128)(2,1)} %param.7, f32[2048]{0:T(1024)S(1)} %convert_element_type.40, f32[128]{0:T(128)S(1)} %add_rsqrt_fusion), kind=kOutput, calls=%fused_computation.27 | convolution fusion | flops 1007927296 | bytes 8888832 | tf_op jit(solution)/shard_map/dot_general | solution.py:23
  93.2 0.7 slice.35
  93.9 32.5 %all-gather = bf16[1,512,640]{2,1,0:T(8,128)(2,1)S(1)} all-gather(bf16[1,64,640]{2,1,0:T(8,128)(2,1)S(1)} %copy-done), channel_id=2, replica_groups=mesh['group'=4,'seq'=8] {'seq'}, dimensions={1}, use_global_device_ids=true | all-gather | bytes 737280 | tf_op jit(solution)/shard_map/all_gather | solution.py:85
  127.0 19.3 %all-gather.1 = s32[1,1024]{1,0:T(1,128)S(1)} all-gather(s32[1,128]{1,0:T(1,128)S(1)} %copy-done.1), channel_id=3, replica_groups=mesh['group'=4,'seq'=8] {'seq'}, dimensions={1}, use_global_device_ids=true | all-gather | bytes 4608 | tf_op jit(solution)/shard_map/all_gather | solution.py:97
  146.3 0.2 copy.14
  146.5 1.0 bitcast_reduce_fusion
  147.5 1.3 fusion.19
  148.9 1.4 fusion.27
  150.3 11.3 %while.18 = (s32[]{:T(128)}, f32[128,5,4]{0,2,1:T(4,128)S(1)}, f32[128,5,4]{0,2,1:T(4,128)S(1)}, f32[128,5,4,64]{0,3,2,1:T(8,128)S(1)}, s32[1024]{0:T(1024)S(1)}...) while((s32[]{:T(128)}, f32[128,5,4]{0,2,1:T(4,128)S(1)}, ...), condition=%wide.region_6.7_spmd.clone, body=%wide.region_3.6_spmd.clone.sunk | while | flops 353113728 | bytes 21081812 | solution.py:72
  150.4 0.2 compare_and_fusion.2
  150.6 1.4 fusion.60
  152.4 0.9 fusion.61
  153.3 1.2 fusion.62
  154.6 1.4 fusion.63
  156.1 0.2 compare_and_fusion.2
  156.3 1.4 fusion.60
  158.0 0.9 fusion.61
  159.0 1.2 fusion.62
  160.2 1.4 fusion.63
  161.7 0.9 copy.18
  (32 shorter events, 1.7 us)
Async XLA Ops:
  6.5 81.9 %all-gather.5.cloned.1.call-start = ((), (), s32[]{:S(2)}) async-start(), calls=%async_computation | async-start | bytes 8110080 | tf_op jit(solution)/shard_map/all_gather | solution.py:25
  7.3 143.1 %all-gather.7.cloned.1.call-start = ((), (), s32[]{:S(2)}) async-start(), calls=%async_computation.1 | async-start | bytes 1474560 | tf_op jit(solution)/shard_map/all_gather | solution.py:96
  9.2 84.6 %copy-start = (bf16[1,64,640]{2,1,0:T(8,128)(2,1)S(1)}, bf16[1,64,640]{2,1,0:T(8,128)(2,1)}, u32[]{:S(2)}) copy-start(bf16[1,64,640]{2,1,0:T(8,128)(2,1)} %param.10) | copy-start | bytes 245764
  9.2 117.7 %copy-start.1 = (s32[1,128]{1,0:T(1,128)S(1)}, s32[1,128]{1,0:T(1,128)}, u32[]{:S(2)}) copy-start(s32[1,128]{1,0:T(1,128)} %param.11) | copy-start | bytes 1540
Sparse Core Ops, SparseCore 0:
  10.3 78.1 all-gather.4
  94.0 42.5 all-gather.6
where the time goes:
time: 170 us; the launch traced here: 169 us
  waiting for transfers between devices  79.9 us (47%)
  blocking collectives  51.8 us (30%)
  between operations  13.5 us (8%)
  matrix products  11.8 us (7%)
  other arithmetic  6.27 us (4%)
  local copies, waits for them, and re-layouts  5.95 us (4%)
    all_gather x1, waiting for transfers between devices, body(): lax.all_gather(w_qkv, ('group', 'seq'), axis=0, tiled=True)  79.2 us
    all_gather x1, blocking collectives, body(): lax.all_gather(prefix_kv[0], 'seq', axis=0, tiled=True)  32.5 us
    all_gather x1, blocking collectives, body(): key_seg = lax.all_gather(seg_ids, 'seq', axis=0, tiled=True)  19.3 us
    dot_general x1, matrix products, body(): jnp.dot(normed, lax.all_gather(w_qkv, ('group', 'seq'), axis=0, tiled=Tru...  4.72 us
    dot_general x3, matrix products, absorb(): jnp.einsum('tgrn,ngd->tgrd', probability.astype(jnp.bfloat16), value_part...  4.22 us
    reduce_sum x3, other arithmetic, absorb(): denominator = denominator * factor + jnp.sum(probability, axis=-1)  3.76 us
  transfers between devices with their start and end apart: 2, of which 1 were waited for; matrix products, arithmetic and copies ran while one was open for 4% of the time, Pallas kernels for 0%

commit v1 on v0

--- a/solution.py
+++ b/solution.py
@@ -94,7 +94,12 @@
         return (seg_block[None, :] == seg_ids[:, None]) & (key_pos[None, :] <= query_pos[:, None])
 
     keyvals = lax.all_gather(local_kv, "seq", axis=0, tiled=True)
-    key_seg = lax.all_gather(seg_ids, "seq", axis=0, tiled=True)
+    ring = [seg_ids]
+    for hop in range(7):
+        ring.append(lax.ppermute(ring[-1], "seq", [(dev, (dev + 1) % 8) for dev in range(8)]))
+    key_seg = jnp.roll(
+        jnp.concatenate(ring[::-1], axis=0), (lax.axis_index("seq") + 1) * ring[0].shape[0], axis=0
+    )
     softmax_state = sweep_keys(softmax_state, keyvals, key_seg, jnp.int32(0), causal_rows)
     running_max, denominator, numerator = softmax_state
     context = (numerator / denominator[..., None]).reshape(row_count, QW).astype(jnp.bfloat16)

time: 170 us -> 156 us (0.918)
  blocking collectives: 51.8 us -> 33.2 us
  starting transfers between devices: 0.04 us -> 3.08 us
    all_gather x1, waiting for transfers between devices: 79.2 us -> 8.48 us  [body(): lax.all_gather(w_qkv, ('group', 'seq'), axis=0, tiled=True)]
    all_gather x1, waiting for transfers between devices: 0.02 us -> 36.3 us  [body(): keyvals = lax.all_gather(local_kv, 'seq', axis=0, tiled=True)]
    ppermute x0 -> x7, waiting for transfers between devices: none -> 35 us  [body(): lax.ppermute(ring[-1], 'seq', [(dev, (dev + 1) % 8) for dev in range(8)])]
    all_gather x1 -> x0, blocking collectives: 19.3 us -> none  [body(): key_seg = lax.all_gather(seg_ids, 'seq', axis=0, tiled=True)]
    ppermute x0 -> x7, starting transfers between devices: none -> 3.04 us  [body(): lax.ppermute(ring[-1], 'seq', [(dev, (dev + 1) % 8) for dev in range(8)])]
  transfers between devices with their start and end apart: 2 -> 9, of which waited for: 1 -> 8; matrix products, arithmetic and copies ran while one was open for 4% -> 5% of each run, Pallas kernels for 0% -> 0%
where the time goes in v1:
time: 156 us; the launch traced here: 155 us
  waiting for transfers between devices  80.5 us (52%)
  blocking collectives  33.2 us (21%)
  between operations  13.6 us (9%)
  matrix products  11.8 us (8%)
  local copies, waits for them, and re-layouts  6.79 us (4%)
  other arithmetic  6.26 us (4%)
  starting transfers between devices  3.08 us (2%)
    all_gather x1, waiting for transfers between devices, body(): keyvals = lax.all_gather(local_kv, 'seq', axis=0, tiled=True)  36.3 us
    ppermute x7, waiting for transfers between devices, body(): lax.ppermute(ring[-1], 'seq', [(dev, (dev + 1) % 8) for dev in range(8)])  35 us
    all_gather x1, blocking collectives, body(): lax.all_gather(prefix_kv[0], 'seq', axis=0, tiled=True)  33.2 us
    all_gather x1, waiting for transfers between devices, body(): lax.all_gather(w_qkv, ('group', 'seq'), axis=0, tiled=True)  8.48 us
    dot_general x1, matrix products, body(): jnp.dot(normed, lax.all_gather(w_qkv, ('group', 'seq'), axis=0, tiled=Tru...  4.72 us
    dot_general x3, matrix products, absorb(): jnp.einsum('tgrn,ngd->tgrd', probability.astype(jnp.bfloat16), value_part...  4.22 us
    reduce_sum x3, other arithmetic, absorb(): denominator = denominator * factor + jnp.sum(probability, axis=-1)  3.76 us
  transfers between devices with their start and end apart: 9, of which 8 were waited for; matrix products, arithmetic and copies ran while one was open for 5% of the time, Pallas kernels for 0%

profile of v1, /device:TPU:0, one launch (start us, length us, event | category | flops | bytes accessed | tf_op | source)
XLA Modules:
  0.0 155.4 jit_solution(686209857335846115)
XLA Ops:
  7.3 3.0 %collective-permute-start = (s32[128]{0:T(128)}, s32[128]{0:T(128)S(1)}, u32[]{:S(2)}, u32[]{:S(2)}) collective-permute-start(s32[128]{0:T(128)} %bitcast.106), channel_id=1, source_target_pairs={{0,1},{1,2},{2,3},{3,4},{4,5},{5,6},{6,7},{7,0},{8,9},{9,10},{10,1... | collective-permute-start | bytes 1544 | tf_op jit(solution)/shard_map/ppermute | solution.py:99
  10.3 33.2 %all-gather = bf16[1,512,640]{2,1,0:T(8,128)(2,1)S(1)} all-gather(bf16[1,64,640]{2,1,0:T(8,128)(2,1)} %param.10), channel_id=2, replica_groups=mesh['group'=4,'seq'=8] {'seq'}, dimensions={1}, use_global_device_ids=true | all-gather | bytes 737280 | tf_op jit(solution)/shard_map/all_gather | solution.py:85
  43.8 6.0 %collective-permute-done.1 = s32[128]{0:T(128)S(1)} collective-permute-done((s32[128]{0:T(128)S(1)}, s32[128]{0:T(128)S(1)}, u32[]{:S(2)}, u32[]{:S(2)}) %collective-permute-start.1) | collective-permute-done | bytes 544 | tf_op jit(solution)/shard_map/ppermute | solution.py:99
  49.8 1.2 fusion.30
  51.0 5.0 %collective-permute-done.2 = s32[128]{0:T(128)S(1)} collective-permute-done((s32[128]{0:T(128)S(1)}, s32[128]{0:T(128)S(1)}, u32[]{:S(2)}, u32[]{:S(2)}) %collective-permute-start.2) | collective-permute-done | bytes 544 | tf_op jit(solution)/shard_map/ppermute | solution.py:99
  56.1 6.2 %collective-permute-done.3 = s32[128]{0:T(128)S(1)} collective-permute-done((s32[128]{0:T(128)S(1)}, s32[128]{0:T(128)S(1)}, u32[]{:S(2)}, u32[]{:S(2)}) %collective-permute-start.3) | collective-permute-done | bytes 544 | tf_op jit(solution)/shard_map/ppermute | solution.py:99
  62.3 6.2 %collective-permute-done.4 = s32[128]{0:T(128)S(1)} collective-permute-done((s32[128]{0:T(128)S(1)}, s32[128]{0:T(128)S(1)}, u32[]{:S(2)}, u32[]{:S(2)}) %collective-permute-start.4) | collective-permute-done | bytes 544 | tf_op jit(solution)/shard_map/ppermute | solution.py:99
  68.5 6.2 %collective-permute-done.5 = s32[128]{0:T(128)S(1)} collective-permute-done((s32[128]{0:T(128)S(1)}, s32[128]{0:T(128)S(1)}, u32[]{:S(2)}, u32[]{:S(2)}) %collective-permute-start.5) | collective-permute-done | bytes 544 | tf_op jit(solution)/shard_map/ppermute | solution.py:99
  75.8 5.2 %collective-permute-done.6 = s32[128]{0:T(128)S(1)} collective-permute-done((s32[128]{0:T(128)S(1)}, s32[128]{0:T(128)S(1)}, u32[]{:S(2)}, u32[]{:S(2)}) %collective-permute-start.6) | collective-permute-done | bytes 544 | tf_op jit(solution)/shard_map/ppermute | solution.py:99
  81.8 8.5 %all-gather.4.cloned.1.call-done = bf16[2048,1920]{1,0:T(8,128)(2,1)} async-done(((bf16[64,1920]{1,0:T(8,128)(2,1)}), bf16[2048,1920]{1,0:T(8,128)(2,1)}) %all-gather.4.cloned.1.call-update) | async-done | bytes 7864336 | tf_op jit(solution)/shard_map/all_gather | solution.py:25
  90.3 4.7 %convolution_convert_fusion = bf16[128,1920]{1,0:T(8,128)(2,1)S(1)} fusion(bf16[2048,1920]{1,0:T(8,128)(2,1)} %all-gather.4.cloned.1.call-done, bf16[1,128,2048]{2,1,0:T(8,128)(2,1)} %param.7, f32[2048]{0:T(1024)S(1)} %convert_element_type.40, f32[128]{0:T(128)S(1)} %add_rsqrt_fusion), kind=kOutput, calls=%fused_computation.27 | convolution fusion | flops 1007927296 | bytes 8888832 | tf_op jit(solution)/shard_map/dot_general | solution.py:23
  96.1 1.0 bitcast_reduce_fusion
  97.1 1.3 fusion.19
  98.5 1.4 fusion.27
  99.9 36.3 %all-gather.6.cloned.1.call-done = bf16[1024,640]{1,0:T(8,128)(2,1)} async-done(((bf16[128,640]{1,0:T(8,128)(2,1)}), bf16[1024,640]{1,0:T(8,128)(2,1)}) %all-gather.6.cloned.1.call-update) | async-done | bytes 1310736 | tf_op jit(solution)/shard_map/all_gather | solution.py:96
  136.2 11.3 %while.18 = (s32[]{:T(128)}, f32[128,5,4]{0,2,1:T(4,128)S(1)}, f32[128,5,4]{0,2,1:T(4,128)S(1)}, f32[128,5,4,64]{0,3,2,1:T(8,128)S(1)}, s32[1024]{0:T(1024)S(1)}...) while((s32[]{:T(128)}, f32[128,5,4]{0,2,1:T(4,128)S(1)}, ...), condition=%wide.region_6.7_spmd.clone, body=%wide.region_3.6_spmd.clone.sunk | while | flops 353113728 | bytes 21081812 | solution.py:72
  136.5 1.4 fusion.60
  138.2 0.9 fusion.61
  139.2 1.2 fusion.62
  140.4 1.4 fusion.63
  142.2 1.4 fusion.60
  143.9 0.9 fusion.61
  144.8 1.2 fusion.62
  146.1 1.4 fusion.63
  (61 shorter events, 6.1 us)
Async XLA Ops:
  6.5 83.7 %all-gather.4.cloned.1.call-start = ((), (), s32[]{:S(2)}) async-start(), calls=%async_computation | async-start | bytes 8110080 | tf_op jit(solution)/shard_map/all_gather | solution.py:25
  7.3 129.0 %all-gather.6.cloned.1.call-start = ((), (), s32[]{:S(2)}) async-start(), calls=%async_computation.1 | async-start | bytes 1474560 | tf_op jit(solution)/shard_map/all_gather | solution.py:96
  7.3 36.3 %collective-permute-start = (s32[128]{0:T(128)}, s32[128]{0:T(128)S(1)}, u32[]{:S(2)}, u32[]{:S(2)}) collective-permute-start(s32[128]{0:T(128)} %bitcast.106), channel_id=1, source_target_pairs={{0,1},{1,2},{2,3},{3,4},{4,5},{5,6},{6,7},{7,0},{8,9},{9,10},{10,1... | collective-permute-start | bytes 1544 | tf_op jit(solution)/shard_map/ppermute | solution.py:99
  43.6 6.2 %collective-permute-start.1 = (s32[128]{0:T(128)S(1)}, s32[128]{0:T(128)S(1)}, u32[]{:S(2)}, u32[]{:S(2)}) collective-permute-start(s32[128]{0:T(128)S(1)} %collective-permute-done), channel_id=1, source_target_pairs={{0,1},{1,2},{2,3},{3,4},{4,5},{5,6},{6,7},{7,0},{8,9},{9,10},{10,1... | collective-permute-start | bytes 1544 | tf_op jit(solution)/shard_map/ppermute | solution.py:99
  49.8 6.2 %collective-permute-start.2 = (s32[128]{0:T(128)S(1)}, s32[128]{0:T(128)S(1)}, u32[]{:S(2)}, u32[]{:S(2)}) collective-permute-start(s32[128]{0:T(128)S(1)} %collective-permute-done.1), channel_id=1, source_target_pairs={{0,1},{1,2},{2,3},{3,4},{4,5},{5,6},{6,7},{7,0},{8,9},{9,10},{10,1... | collective-permute-start | bytes 1544 | tf_op jit(solution)/shard_map/ppermute | solution.py:99
  56.1 6.2 %collective-permute-start.3 = (s32[128]{0:T(128)S(1)}, s32[128]{0:T(128)S(1)}, u32[]{:S(2)}, u32[]{:S(2)}) collective-permute-start(s32[128]{0:T(128)S(1)} %collective-permute-done.2), channel_id=1, source_target_pairs={{0,1},{1,2},{2,3},{3,4},{4,5},{5,6},{6,7},{7,0},{8,9},{9,10},{10,1... | collective-permute-start | bytes 1544 | tf_op jit(solution)/shard_map/ppermute | solution.py:99
  62.3 6.2 %collective-permute-start.4 = (s32[128]{0:T(128)S(1)}, s32[128]{0:T(128)S(1)}, u32[]{:S(2)}, u32[]{:S(2)}) collective-permute-start(s32[128]{0:T(128)S(1)} %collective-permute-done.3), channel_id=1, source_target_pairs={{0,1},{1,2},{2,3},{3,4},{4,5},{5,6},{6,7},{7,0},{8,9},{9,10},{10,1... | collective-permute-start | bytes 1544 | tf_op jit(solution)/shard_map/ppermute | solution.py:99
  68.5 6.2 %collective-permute-start.5 = (s32[128]{0:T(128)S(1)}, s32[128]{0:T(128)S(1)}, u32[]{:S(2)}, u32[]{:S(2)}) collective-permute-start(s32[128]{0:T(128)S(1)} %collective-permute-done.4), channel_id=1, source_target_pairs={{0,1},{1,2},{2,3},{3,4},{4,5},{5,6},{6,7},{7,0},{8,9},{9,10},{10,1... | collective-permute-start | bytes 1544 | tf_op jit(solution)/shard_map/ppermute | solution.py:99
  74.8 6.2 %collective-permute-start.6 = (s32[128]{0:T(128)S(1)}, s32[128]{0:T(128)S(1)}, u32[]{:S(2)}, u32[]{:S(2)}) collective-permute-start(s32[128]{0:T(128)S(1)} %collective-permute-done.5), channel_id=1, source_target_pairs={{0,1},{1,2},{2,3},{3,4},{4,5},{5,6},{6,7},{7,0},{8,9},{9,10},{10,1... | collective-permute-start | bytes 1544 | tf_op jit(solution)/shard_map/ppermute | solution.py:99
  81.8 14.0 %copy-start = (s32[1,128]{1,0:T(1,128)S(1)}, s32[1,128]{1,0:T(1,128)}, u32[]{:S(2)}) copy-start(s32[1,128]{1,0:T(1,128)} %param.11) | copy-start | bytes 1540
Sparse Core Ops, SparseCore 0:
  10.3 79.9 all-gather.3
  95.8 40.3 all-gather.5
